TPU v7x, 128 devices: a whole 4x4x4 slice. The times are simulated.
128 devices in a mesh: sec: 2 (over z_lo), row: 8 (over x, z_hi), col: 8 (over y, core).
Axes of the slice: x: 4, y: 4, z: 4 (z_hi: 2, z_lo: 2; z = z_hi * 2 + z_lo), core: 2. Of those that a mesh axis runs over, the one named last changes fastest.
Arguments:
- held_inverse: bfloat16 [12288, 12288], P('row', ('sec', 'col')), as said below
- factor_panels: bfloat16 [2, 12288, 1024], P(None, ('sec', 'col'), 'row'), may hold values from -0.125 to 0.125
- block_inverses: bfloat16 [2, 1024, 1024], P(None, 'row'), as said below
- covariance: float32 [12288, 12288], P('row', ('sec', 'col')), may hold values from -0.9 to 0.9
Outputs:
- updated: float32 [12288, 12288], P('row', ('sec', 'col'))
Inputs may be any that keep to these rules, and one draw needn't show every extreme that they name: held_inverse is lower triangular with a positive diagonal. Each block of block_inverses is lower triangular with a positive diagonal.
All inputs are finite; a program needn't handle non-finite values.
Results may differ from a plain program's by a relative error of at most 0.0038.
Values may be sent and summed in bfloat16 or wider, within the bound.
A program may use at most 128 MiB of HBM per device.

v0:
```python
import jax
import jax.numpy as jnp
from jax import lax
from jax.sharding import Mesh
from jax.sharding import PartitionSpec as P

PANELS = 2
ROW = ("row_0", "row_1")


def scatter_axes(x, axes, dim):
    for axis in axes:
        x = lax.psum_scatter(x, axis, scatter_dimension=dim, tiled=True)
    return x


def from_root(x, axis, root):
    mine = lax.axis_index(axis) == root
    return lax.psum(jnp.where(mine, x, jnp.zeros_like(x)), axis)


def body(held_inverse, factor_panels, block_inverses, covariance):
    total = covariance
    tile_cols = held_inverse.shape[1]
    groups = lax.axis_size(("sec", "col"))
    ratio = groups // lax.axis_size(ROW)
    column_index = lax.axis_index(("sec", "col"))
    root_row = column_index // ratio
    offset = column_index % ratio * tile_cols
    for panel in range(PANELS):
        partial_value = jnp.dot(
            factor_panels[panel], block_inverses[panel], preferred_element_type=jnp.float32
        )
        scaled = scatter_axes(partial_value, ROW, 1).astype(jnp.bfloat16)
        terms = jnp.dot(
            held_inverse,
            lax.all_gather(scaled, ROW, axis=1, tiled=True),
            preferred_element_type=jnp.float32,
        )
        summed = lax.psum(terms, ("sec", "col"))
        inverse = (-summed).astype(jnp.bfloat16)
        own_block = lax.dynamic_slice_in_dim(inverse, offset, tile_cols, 0)
        column_block = from_root(own_block, ROW, root_row)
        total = total + lax.dot_general(
            inverse, column_block, (((1,), (1,)), ((), ())), preferred_element_type=jnp.float32
        )
    return total


def solution(mesh):
    split = Mesh(
        mesh.devices.reshape(mesh.shape["sec"], 4, 2, mesh.shape["col"]),
        ("sec", "row_0", "row_1", "col"),
    )
    in_specs = (
        P(ROW, ("sec", "col")),
        P(None, ("sec", "col"), ROW),
        P(None, ROW, None),
        P(ROW, ("sec", "col")),
    )
    out_specs = P(ROW, ("sec", "col"))
    return jax.shard_map(body, mesh=split, in_specs=in_specs, out_specs=out_specs, check_vma=False)
```

profile of v0, /device:TPU:5, one launch (start us, length us, event | category | flops | bytes accessed | tf_op | source)
XLA Modules:
  0.0 585.9 jit_solution(17937898365134801965)
XLA Ops:
  6.5 0.0 copy-start
  6.5 0.0 copy-start.4
  6.5 0.0 copy-start.5
  6.5 0.0 reduce-scatter.5.cloned.1.call-start
  6.5 3.4 fusion.2
  10.0 0.0 reduce-scatter.5.cloned.1.call-update
  10.0 0.0 reduce-scatter.9.cloned.1.call-start
  10.0 0.0 copy-done.4
  10.0 0.0 copy-done.5
  10.1 2.2 fusion
  12.3 0.0 reduce-scatter.9.cloned.1.call-update
  12.3 0.0 reduce-scatter.7.cloned.1.call-start
  12.3 36.8 %reduce-scatter.5.cloned.1.call-done = f32[768,256]{1,0:T(8,128)} async-done(((f32[768,1024]{1,0:T(8,128)}), f32[768,256]{1,0:T(8,128)}) %reduce-scatter.5.cloned.1.call-update) | async-done | bytes 786448 | tf_op jit(solution)/shard_map/reduce_scatter | solution.py:13
  49.2 0.0 reduce-scatter.7.cloned.1.call-update
  49.2 0.0 reduce-scatter.11.cloned.1.call-start
  49.2 40.3 %reduce-scatter.9.cloned.1.call-done = f32[768,256]{1,0:T(8,128)} async-done(((f32[768,1024]{1,0:T(8,128)}), f32[768,256]{1,0:T(8,128)}) %reduce-scatter.9.cloned.1.call-update) | async-done | bytes 786448 | tf_op jit(solution)/shard_map/reduce_scatter | solution.py:13
  89.6 0.0 reduce-scatter.11.cloned.1.call-update
  89.6 0.0 all-gather.3.cloned.1.call-start
  89.6 25.2 %reduce-scatter.7.cloned.1.call-done = f32[768,128]{1,0:T(8,128)} async-done(((f32[768,256]{1,0:T(8,128)}), f32[768,128]{1,0:T(8,128)}) %reduce-scatter.7.cloned.1.call-update) | async-done | bytes 393232 | tf_op jit(solution)/shard_map/reduce_scatter | solution.py:13
  114.8 1.7 convert_element_type.12
  116.5 0.0 all-gather.3.cloned.1.call-update
  116.6 0.0 all-gather.5.cloned.1.call-start
  116.6 21.3 %reduce-scatter.11.cloned.1.call-done = f32[768,128]{1,0:T(8,128)} async-done(((f32[768,256]{1,0:T(8,128)}), f32[768,128]{1,0:T(8,128)}) %reduce-scatter.11.cloned.1.call-update) | async-done | bytes 393232 | tf_op jit(solution)/shard_map/reduce_scatter | solution.py:13
  138.0 1.7 convert_element_type.14
  139.7 0.0 all-gather.5.cloned.1.call-update
  139.7 0.0 all-reduce.5.cloned.1.call-start
  139.7 49.3 %all-gather.3.cloned.1.call-done = bf16[768,1024]{1,0:T(8,128)(2,1)} async-done(((bf16[768,128]{1,0:T(8,128)(2,1)}), bf16[768,1024]{1,0:T(8,128)(2,1)}) %all-gather.3.cloned.1.call-update) | async-done | bytes 1572880 | tf_op jit(solution)/shard_map/all_gather | solution.py:37
  189.0 0.0 copy-done
  189.0 6.1 %convolution_bitcast_fusion.1 = f32[1536,1024]{0,1:T(8,128)} fusion(bf16[768,1024]{1,0:T(8,128)(2,1)} %all-gather.3.cloned.1.call-done, bf16[1536,768]{1,0:T(8,128)(2,1)S(1)} %copy-done), kind=kOutput, calls=%fused_computation.4 | convolution fusion | flops 2415919104 | bytes 10223616 | tf_op jit(solution)/shard_map/dot_general | solution.py:35
  195.2 47.0 %all-gather.5.cloned.1.call-done = bf16[768,1024]{1,0:T(8,128)(2,1)} async-done(((bf16[768,128]{1,0:T(8,128)(2,1)}), bf16[768,1024]{1,0:T(8,128)(2,1)}) %all-gather.5.cloned.1.call-update) | async-done | bytes 1572880 | tf_op jit(solution)/shard_map/all_gather | solution.py:37
  242.1 6.0 %convolution_bitcast_fusion = f32[1536,1024]{0,1:T(8,128)} fusion(bf16[768,1024]{1,0:T(8,128)(2,1)} %all-gather.5.cloned.1.call-done, bf16[1536,768]{1,0:T(8,128)(2,1)S(1)} %copy-done), kind=kOutput, calls=%fused_computation.3 | convolution fusion | flops 2415919104 | bytes 10223616 | tf_op jit(solution)/shard_map/dot_general | solution.py:35
  248.1 0.0 all-reduce.5.cloned.1.call-update
  248.1 0.0 all-reduce.7.cloned.1.call-start
  248.2 159.2 %all-reduce.5.cloned.1.call-done = (f32[1536,1024]{0,1:T(8,128)}, f32[1536,1024]{0,1:T(8,128)}) async-done(((f32[1536,1024]{0,1:T(8,128)}, f32[1536,1024]{0,1:T(8,128)}), (f32[1536,1024]{0,1:T(8,128)}, f32[1536,1024]{0,1:T(8,128)})) %all-reduce.5.cloned.1.call-update) | async-done | bytes 12582928 | tf_op jit(solution)/shard_map/psum | solution.py:40
  407.4 6.3 %negate_convert_fusion = (bf16[1536,1024]{0,1:T(8,128)(2,1)S(1)}, bf16[1536,1024]{0,1:T(8,128)(2,1)S(1)}) fusion(f32[1536,1024]{0,1:T(8,128)} %get-tuple-element.6, f32[1536,1024]{0,1:T(8,128)} %get-tuple-element.5), kind=kLoop, calls=%fused_computation | loop fusion | flops 6291456 | bytes 18874368 | tf_op jit(solution)/shard_map/convert_element_type | solution.py:41
  413.7 0.0 copy-start.2
  413.7 1.7 dynamic-slice_select_fusion.1
  415.4 0.4 copy-done.2
  415.9 1.5 dynamic-slice_select_fusion
  417.4 0.0 all-reduce.7.cloned.1.call-update
  417.4 151.0 %all-reduce.7.cloned.1.call-done = (bf16[768,1024]{0,1:T(8,128)(2,1)}, bf16[768,1024]{0,1:T(8,128)(2,1)}) async-done(((bf16[768,1024]{0,1:T(8,128)(2,1)}, bf16[768,1024]{0,1:T(8,128)(2,1)}), (bf16[768,1024]{0,1:T(8,128)(2,1)}, bf16[768,1024]{0,1:T(8,128)(2,1)})) %all-reduce.7.cloned.1.call-update) | async-done | bytes 3145744 | tf_op jit(solution)/shard_map/psum | solution.py:19
  568.4 0.0 copy-start.3
  568.4 4.3 fusion.10
  572.7 0.0 copy-done.3
  572.7 0.0 copy-done.6
  572.7 0.0 copy-start.1
  572.7 6.4 %add_add_fusion = f32[1536,768]{1,0:T(8,128)} fusion(f32[1536,768]{1,0:T(8,128)} %param.7, f32[1536,768]{1,0:T(8,128)S(1)} %fusion.10, bf16[1536,1024]{0,1:T(8,128)(2,1)S(1)} %copy-done.3, bf16[768,1024]{0,1:T(8,128)(2,1)S(1)} %copy-done.6), kind=kOutput, calls=%fused_computation.2 | convolution fusion | flops 2418278400 | bytes 18874368 | tf_op jit(solution)/shard_map/dot_general | solution.py:44
  579.1 0.0 copy-done.1
  (1 shorter events, 0.0 us)
Async XLA Ops:
  6.5 182.5 %copy-start = (bf16[1536,768]{1,0:T(8,128)(2,1)S(1)}, bf16[1536,768]{1,0:T(8,128)(2,1)}, u32[]{:S(2)}) copy-start(bf16[1536,768]{1,0:T(8,128)(2,1)} %param.4) | copy-start | bytes 7077892
  6.5 3.5 copy-start.4
  6.5 3.5 copy-start.5
  6.5 42.6 %reduce-scatter.5.cloned.1.call-start = ((), (), s32[]{:S(2)}) async-start(), calls=%async_computation.4 | async-start | bytes 3932160 | tf_op jit(solution)/shard_map/reduce_scatter | solution.py:13
  10.0 79.6 %reduce-scatter.9.cloned.1.call-start = ((), (), s32[]{:S(2)}) async-start(), calls=%async_computation.7 | async-start | bytes 3932160 | tf_op jit(solution)/shard_map/reduce_scatter | solution.py:13
  12.3 102.6 %reduce-scatter.7.cloned.1.call-start = ((), (), s32[]{:S(2)}) async-start(), calls=%async_computation.5 | async-start | bytes 1179648 | tf_op jit(solution)/shard_map/reduce_scatter | solution.py:13
  49.2 88.8 %reduce-scatter.11.cloned.1.call-start = ((), (), s32[]{:S(2)}) async-start(), calls=%async_computation.8 | async-start | bytes 1179648 | tf_op jit(solution)/shard_map/reduce_scatter | solution.py:13
  89.6 99.4 %all-gather.3.cloned.1.call-start = ((), (), s32[]{:S(2)}) async-start(), calls=%async_computation.6 | async-start | bytes 1769472 | tf_op jit(solution)/shard_map/all_gather | solution.py:37
  116.6 125.6 %all-gather.5.cloned.1.call-start = ((), (), s32[]{:S(2)}) async-start(), calls=%async_computation.9 | async-start | bytes 1769472 | tf_op jit(solution)/shard_map/all_gather | solution.py:37
  139.7 267.7 %all-reduce.5.cloned.1.call-start = ((), (), s32[]{:S(2)}) async-start(), calls=%async_computation.10 | async-start | bytes 25165824 | tf_op jit(solution)/shard_map/psum | solution.py:40
  248.1 320.3 %all-reduce.7.cloned.1.call-start = ((), (), s32[]{:S(2)}) async-start(), calls=%async_computation.11 | async-start | bytes 6291456 | tf_op jit(solution)/shard_map/psum | solution.py:19
  413.7 2.2 copy-start.2
  568.4 4.3 copy-start.3
  568.4 4.3 copy-start.6
  572.7 6.4 %copy-start.1 = (bf16[1536,768]{1,0:T(8,128)(2,1)S(1)}, bf16[1536,768]{1,0:T(8,128)(2,1)}, u32[]{:S(2)}) copy-start(bf16[1536,768]{1,0:T(8,128)(2,1)} %param.4) | copy-start | bytes 7077892
Sparse Core Ops, SparseCore 0:
  10.1 38.9 reduce-scatter.4
  51.6 37.9 reduce-scatter.8
  91.9 22.8 reduce-scatter.6
  117.0 20.8 reduce-scatter.10
  140.0 48.9 all-gather.2
  191.0 51.0 all-gather.4
  248.2 159.1 all-reduce.4
  417.5 150.8 all-reduce.6
where the time goes:
time: 586 us
  waiting for transfers between devices  530 us (90%)
  matrix products  28.4 us (5%)
  between operations  13.6 us (2%)
  other arithmetic  12.9 us (2%)
    psum x1, waiting for transfers between devices, body(): summed = lax.psum(terms, ('sec', 'col'))  159 us
    psum x1, waiting for transfers between devices, from_root(): return lax.psum(jnp.where(mine, x, jnp.zeros_like(x)), axis)  151 us
    reduce_scatter x4, waiting for transfers between devices, scatter_axes(): x = lax.psum_scatter(x, axis, scatter_dimension=dim, tiled=True)  124 us
    all_gather x2, waiting for transfers between devices, body(): lax.all_gather(scaled, ROW, axis=1, tiled=True)  96.2 us
    dot_general x2, matrix products, body(): jnp.dot(held_inverse, lax.all_gather(scaled, ROW, axis=1, tiled=True), pr...  12.1 us
  transfers between devices with their start and end apart: 8, of which 8 were waited for; matrix products, arithmetic and copies ran while one was open for 2% of the time, Pallas kernels for 0%

commit v1 on v0

--- a/solution.py
+++ b/solution.py
@@ -34,7 +34,9 @@
         scaled = scatter_axes(partial_value, ROW, 1).astype(jnp.bfloat16)
         terms = jnp.dot(
             held_inverse,
-            lax.all_gather(scaled, ROW, axis=1, tiled=True),
+            jnp.concatenate(
+                lax.all_to_all(jnp.stack([scaled] * lax.axis_size(ROW)), ROW, 0, 0), axis=1
+            ),
             preferred_element_type=jnp.float32,
         )
         summed = lax.psum(terms, ("sec", "col"))

time: 586 us -> 524 us (0.89)
  waiting for transfers between devices: 530 us -> 458 us
  starting transfers between devices: 0.29 us -> 9.07 us
    all_gather x2 -> x0, waiting for transfers between devices: 96.2 us -> none  [body(): lax.all_gather(scaled, ROW, axis=1, tiled=True)]
    all_to_all x0 -> x2, waiting for transfers between devices: none -> 16.4 us  [body(): lax.all_to_all(jnp.stack([scaled] * lax.axis_size(ROW)), ROW, 0, 0)]
    reduce_scatter x4, waiting for transfers between devices: 124 us -> 133 us  [scatter_axes(): x = lax.psum_scatter(x, axis, scatter_dimension=dim, tiled=True)]
    all_to_all x0 -> x2, starting transfers between devices: none -> 8.91 us  [body(): lax.all_to_all(jnp.stack([scaled] * lax.axis_size(ROW)), ROW, 0, 0)]
  transfers between devices with their start and end apart: 8 -> 8, of which waited for: 8 -> 7; matrix products, arithmetic and copies ran while one was open for 2% -> 2% of each run, Pallas kernels for 0% -> 0%
where the time goes in v1:
time: 524 us
  waiting for transfers between devices  458 us (87%)
  matrix products  28.3 us (5%)
  between operations  13.6 us (3%)
  other arithmetic  11.6 us (2%)
  starting transfers between devices  9.07 us (2%)
    psum x1, waiting for transfers between devices, body(): summed = lax.psum(terms, ('sec', 'col'))  158 us
    psum x1, waiting for transfers between devices, from_root(): return lax.psum(jnp.where(mine, x, jnp.zeros_like(x)), axis)  151 us
    reduce_scatter x4, waiting for transfers between devices, scatter_axes(): x = lax.psum_scatter(x, axis, scatter_dimension=dim, tiled=True)  133 us
    all_to_all x2, waiting for transfers between devices, body(): lax.all_to_all(jnp.stack([scaled] * lax.axis_size(ROW)), ROW, 0, 0)  16.4 us
    dot_general x2, matrix products, body(): jnp.dot(held_inverse, jnp.concatenate(lax.all_to_all(jnp.stack([scaled] *...  12 us
    dot_general x2, matrix products, body(): lax.dot_general(inverse, column_block, (((1,), (1,)), ((), ())), preferre...  10.7 us
  transfers between devices with their start and end apart: 8, of which 7 were waited for; matrix products, arithmetic and copies ran while one was open for 2% of the time, Pallas kernels for 0%

profile of v1, /device:TPU:5, one launch (start us, length us, event | category | flops | bytes accessed | tf_op | source)
XLA Modules:
  0.0 523.6 jit_solution(15603161742956009931)
XLA Ops:
  6.5 0.0 copy-start
  6.5 0.0 copy-start.4
  6.5 0.0 reduce-scatter.5.cloned.1.call-start
  6.5 3.4 fusion.2
  10.0 0.0 reduce-scatter.5.cloned.1.call-update
  10.0 0.0 reduce-scatter.9.cloned.1.call-start
  10.0 0.0 copy-done.4
  10.0 0.0 copy-done.5
  10.1 2.2 fusion
  12.3 0.0 reduce-scatter.9.cloned.1.call-update
  12.3 0.0 reduce-scatter.7.cloned.1.call-start
  12.3 36.8 %reduce-scatter.5.cloned.1.call-done = f32[768,256]{1,0:T(8,128)} async-done(((f32[768,1024]{1,0:T(8,128)}), f32[768,256]{1,0:T(8,128)}) %reduce-scatter.5.cloned.1.call-update) | async-done | bytes 786448 | tf_op jit(solution)/shard_map/reduce_scatter | solution.py:13
  49.2 0.0 reduce-scatter.7.cloned.1.call-update
  49.2 0.0 reduce-scatter.11.cloned.1.call-start
  49.2 40.3 %reduce-scatter.9.cloned.1.call-done = f32[768,256]{1,0:T(8,128)} async-done(((f32[768,1024]{1,0:T(8,128)}), f32[768,256]{1,0:T(8,128)}) %reduce-scatter.9.cloned.1.call-update) | async-done | bytes 786448 | tf_op jit(solution)/shard_map/reduce_scatter | solution.py:13
  89.6 0.0 reduce-scatter.11.cloned.1.call-update
  89.6 25.3 %reduce-scatter.7.cloned.1.call-done = f32[768,128]{1,0:T(8,128)} async-done(((f32[768,256]{1,0:T(8,128)}), f32[768,128]{1,0:T(8,128)}) %reduce-scatter.7.cloned.1.call-update) | async-done | bytes 393232 | tf_op jit(solution)/shard_map/reduce_scatter | solution.py:13
  114.8 1.0 convert_element_type.12
  115.9 0.1 copy.5
  116.0 1.2 stack.4
  117.3 4.4 all-to-all-start
  121.7 30.4 %reduce-scatter.11.cloned.1.call-done = f32[768,128]{1,0:T(8,128)} async-done(((f32[768,256]{1,0:T(8,128)}), f32[768,128]{1,0:T(8,128)}) %reduce-scatter.11.cloned.1.call-update) | async-done | bytes 393232 | tf_op jit(solution)/shard_map/reduce_scatter | solution.py:13
  152.1 1.0 convert_element_type.14
  153.2 0.1 copy.6
  153.3 0.0 all-to-all-done
  153.3 1.2 stack.5
  154.6 4.5 all-to-all-start.1
  159.0 0.0 all-reduce.5.cloned.1.call-start
  159.0 0.0 copy-done
  159.1 6.1 %convolution_bitcast_fusion.1 = f32[1536,1024]{0,1:T(8,128)} fusion(bf16[768,1024]{0,1:T(8,128)(2,1)} %bitcast.3, bf16[1536,768]{1,0:T(8,128)(2,1)S(1)} %copy-done), kind=kOutput, calls=%fused_computation.4 | convolution fusion | flops 2415919104 | bytes 10223616 | tf_op jit(solution)/shard_map/dot_general | solution.py:35
  165.1 16.4 %all-to-all-done.1 = bf16[8,768,128]{1,2,0:T(8,128)(2,1)} async-done(((bf16[8,768,128]{1,2,0:T(8,128)(2,1)}), bf16[8,768,128]{1,2,0:T(8,128)(2,1)}, u32[]{:S(2)}, u32[]{:S(2)}) %all-to-all-start.1) | async-done | bytes 1572896 | tf_op jit(solution)/shard_map/all_to_all | solution.py:38
  181.5 6.0 %convolution_bitcast_fusion = f32[1536,1024]{0,1:T(8,128)} fusion(bf16[768,1024]{0,1:T(8,128)(2,1)} %bitcast.8, bf16[1536,768]{1,0:T(8,128)(2,1)S(1)} %copy-done), kind=kOutput, calls=%fused_computation.3 | convolution fusion | flops 2415919104 | bytes 10223616 | tf_op jit(solution)/shard_map/dot_general | solution.py:35
  187.4 0.0 all-reduce.5.cloned.1.call-update
  187.4 0.0 all-reduce.7.cloned.1.call-start
  187.5 157.5 %all-reduce.5.cloned.1.call-done = (f32[1536,1024]{0,1:T(8,128)}, f32[1536,1024]{0,1:T(8,128)}) async-done(((f32[1536,1024]{0,1:T(8,128)}, f32[1536,1024]{0,1:T(8,128)}), (f32[1536,1024]{0,1:T(8,128)}, f32[1536,1024]{0,1:T(8,128)})) %all-reduce.5.cloned.1.call-update) | async-done | bytes 12582928 | tf_op jit(solution)/shard_map/psum | solution.py:42
  345.1 6.3 %negate_convert_fusion = (bf16[1536,1024]{0,1:T(8,128)(2,1)S(1)}, bf16[1536,1024]{0,1:T(8,128)(2,1)S(1)}) fusion(f32[1536,1024]{0,1:T(8,128)} %get-tuple-element.6, f32[1536,1024]{0,1:T(8,128)} %get-tuple-element.5), kind=kLoop, calls=%fused_computation | loop fusion | flops 6291456 | bytes 18874368 | tf_op jit(solution)/shard_map/convert_element_type | solution.py:43
  351.4 0.0 copy-start.2
  351.4 1.7 dynamic-slice_select_fusion.1
  353.1 0.4 copy-done.2
  353.6 1.5 dynamic-slice_select_fusion
  355.1 0.0 all-reduce.7.cloned.1.call-update
  355.1 151.0 %all-reduce.7.cloned.1.call-done = (bf16[768,1024]{0,1:T(8,128)(2,1)}, bf16[768,1024]{0,1:T(8,128)(2,1)}) async-done(((bf16[768,1024]{0,1:T(8,128)(2,1)}, bf16[768,1024]{0,1:T(8,128)(2,1)}), (bf16[768,1024]{0,1:T(8,128)(2,1)}, bf16[768,1024]{0,1:T(8,128)(2,1)})) %all-reduce.7.cloned.1.call-update) | async-done | bytes 3145744 | tf_op jit(solution)/shard_map/psum | solution.py:19
  506.1 4.3 fusion.10
  510.4 0.0 copy-done.3
  510.4 0.0 copy-done.6
  510.4 0.0 copy-start.1
  510.4 6.4 %add_add_fusion = f32[1536,768]{1,0:T(8,128)} fusion(f32[1536,768]{1,0:T(8,128)} %param.7, f32[1536,768]{1,0:T(8,128)S(1)} %fusion.10, bf16[1536,1024]{0,1:T(8,128)(2,1)S(1)} %copy-done.3, bf16[768,1024]{0,1:T(8,128)(2,1)S(1)} %copy-done.6), kind=kOutput, calls=%fused_computation.2 | convolution fusion | flops 2418278400 | bytes 18874368 | tf_op jit(solution)/shard_map/dot_general | solution.py:46
  516.8 0.0 copy-done.1
  (3 shorter events, 0.0 us)
Async XLA Ops:
  6.5 152.5 %copy-start = (bf16[1536,768]{1,0:T(8,128)(2,1)S(1)}, bf16[1536,768]{1,0:T(8,128)(2,1)}, u32[]{:S(2)}) copy-start(bf16[1536,768]{1,0:T(8,128)(2,1)} %param.4) | copy-start | bytes 7077892
  6.5 3.5 copy-start.4
  6.5 3.5 copy-start.5
  6.5 42.6 %reduce-scatter.5.cloned.1.call-start = ((), (), s32[]{:S(2)}) async-start(), calls=%async_computation.6 | async-start | bytes 3932160 | tf_op jit(solution)/shard_map/reduce_scatter | solution.py:13
  10.0 79.6 %reduce-scatter.9.cloned.1.call-start = ((), (), s32[]{:S(2)}) async-start(), calls=%async_computation.8 | async-start | bytes 3932160 | tf_op jit(solution)/shard_map/reduce_scatter | solution.py:13
  12.3 102.5 %reduce-scatter.7.cloned.1.call-start = ((), (), s32[]{:S(2)}) async-start(), calls=%async_computation.7 | async-start | bytes 1179648 | tf_op jit(solution)/shard_map/reduce_scatter | solution.py:13
  49.2 103.0 %reduce-scatter.11.cloned.1.call-start = ((), (), s32[]{:S(2)}) async-start(), calls=%async_computation.9 | async-start | bytes 1179648 | tf_op jit(solution)/shard_map/reduce_scatter | solution.py:13
  117.3 36.1 %all-to-all-start = ((bf16[8,768,128]{1,2,0:T(8,128)(2,1)}), bf16[8,768,128]{1,2,0:T(8,128)(2,1)}, u32[]{:S(2)}, u32[]{:S(2)}) async-start(bf16[8,768,128]{1,2,0:T(8,128)(2,1)} %stack.4), calls=%async_computation.2 | async-start | bytes 3145728 | tf_op jit(solution)/shard_map/all_to_all | solution.py:38
  154.6 26.9 %all-to-all-start.1 = ((bf16[8,768,128]{1,2,0:T(8,128)(2,1)}), bf16[8,768,128]{1,2,0:T(8,128)(2,1)}, u32[]{:S(2)}, u32[]{:S(2)}) async-start(bf16[8,768,128]{1,2,0:T(8,128)(2,1)} %stack.5), calls=%async_computation.5 | async-start | bytes 3145728 | tf_op jit(solution)/shard_map/all_to_all | solution.py:38
  159.0 186.0 %all-reduce.5.cloned.1.call-start = ((), (), s32[]{:S(2)}) async-start(), calls=%async_computation.10 | async-start | bytes 25165824 | tf_op jit(solution)/shard_map/psum | solution.py:42
  187.4 318.6 %all-reduce.7.cloned.1.call-start = ((), (), s32[]{:S(2)}) async-start(), calls=%async_computation.11 | async-start | bytes 6291456 | tf_op jit(solution)/shard_map/psum | solution.py:19
  351.4 2.2 copy-start.2
  506.1 4.3 copy-start.3
  506.1 4.4 copy-start.6
  510.4 6.4 %copy-start.1 = (bf16[1536,768]{1,0:T(8,128)(2,1)S(1)}, bf16[1536,768]{1,0:T(8,128)(2,1)}, u32[]{:S(2)}) copy-start(bf16[1536,768]{1,0:T(8,128)(2,1)} %param.4) | copy-start | bytes 7077892
Sparse Core Ops, SparseCore 0:
  10.1 38.9 reduce-scatter.4
  51.6 37.9 reduce-scatter.8
  91.9 22.8 reduce-scatter.6
  117.0 35.0 reduce-scatter.10
  187.6 157.4 all-reduce.4
  355.2 150.8 all-reduce.6
